TPU v7x, 128 devices: a whole 4x4x4 slice. The times are simulated.
128 devices in a mesh: ctx: 32 (over z, y_lo, x), grp: 4 (over y_hi, core).
Axes of the slice: x: 4, y: 4 (y_hi: 2, y_lo: 2; y = y_hi * 2 + y_lo), z: 4, core: 2. Of those that a mesh axis runs over, the one named last changes fastest.
Arguments:
- query_input: bfloat16 [16384, 4096], P(('ctx', 'grp')), may hold values from -6 to 6
- key_input: bfloat16 [16384, 4096], P(('ctx', 'grp')), may hold values from -6 to 6
- value_input: bfloat16 [16384, 4096], P(('ctx', 'grp')), may hold values from -6 to 6
- out_grad: bfloat16 [16384, 4096], P(('ctx', 'grp')), may hold values from -6 to 6
- residues: float32 [8, 16], replicated, may hold values from -2 to 2
- decay_rates: float32 [8, 16], replicated, may hold values from 3.0517578e-06 to 0.15
Outputs:
- output: float32 [16384, 4096], P(('ctx', 'grp'))
- query_grad: float32 [16384, 4096], P(('ctx', 'grp'))
- key_grad: float32 [16384, 4096], P(('ctx', 'grp'))
- value_grad: float32 [16384, 4096], P(('ctx', 'grp'))
- residue_grad: float32 [8, 16], replicated
All inputs are finite; a program needn't handle non-finite values.
Results may differ from a plain program's by a relative error of at most 0.0055.
Values may be sent and summed in bfloat16 or wider, within the bound.
A program may use at most 192 MiB of HBM per device.

v0:
```python
import math
import jax
import jax.numpy as jnp
from jax import lax
from jax.sharding import PartitionSpec as P

GROUP = 512
HIGHEST = lax.Precision.HIGHEST


def entering(part, axis, combine, identity, reverse):
    count = lax.axis_size(axis)
    place = lax.axis_index(axis)
    ahead = count - 1 - place if reverse else place
    gathered = jax.tree.map(lambda a: lax.all_gather(a, axis), part)
    state = jax.tree.map(lambda a, e: jnp.zeros_like(a) + jnp.asarray(e, a.dtype), part, identity)

    def one(hop, state):
        source = count - 1 - hop if reverse else hop
        return combine(
            state, jax.tree.map(lambda a: lax.dynamic_index_in_dim(a, source, 0, False), gathered)
        )

    return lax.fori_loop(0, ahead, one, state)


def mode_tables(term_residues, decays, pairing, span):
    position = jnp.arange(span).astype(jnp.float32)
    distance = position[:, None] - position[None, :]
    causal_mask = distance >= 0.0
    lag_values = jnp.maximum(distance, 0.0)
    group_count = term_residues.shape[0]

    def one_mode(total, columns):
        res_column, decay_column = columns
        weight = jnp.where(
            causal_mask[None], jnp.exp(-decay_column[:, None, None] * lag_values[None]), 0.0
        )
        total = total + res_column[:, None, None] * weight
        return (total, jnp.sum(pairing * weight, axis=(1, 2)))

    start_total = jnp.zeros((group_count, span, span), jnp.float32)
    causal, inside = lax.scan(one_mode, start_total, (term_residues.T, decays.T))
    upper_part = causal.astype(jnp.bfloat16)
    lower_part = (causal - upper_part.astype(jnp.float32)).astype(jnp.bfloat16)
    return (upper_part, lower_part, inside.T)


def link_states(earlier, later):
    return (later[1][:, :, None] * earlier[0] + later[0], earlier[1] * later[1])


def convolve(product, inner_grad, term_residues, decays, carry_states):
    span, columns = product.shape
    group_count = columns // GROUP
    grouped = product.reshape(span, group_count, GROUP)
    grad_rows = inner_grad.reshape(span, group_count, GROUP)
    pairing = jnp.einsum("agc,bgc->gab", grad_rows, grouped, preferred_element_type=jnp.float32)
    upper_part, lower_part, inside = mode_tables(term_residues, decays, pairing, span)
    mixed_sum = jnp.einsum("gab,bgc->agc", upper_part, grouped, preferred_element_type=jnp.float32)
    mixed_sum = mixed_sum + jnp.einsum(
        "gab,bgc->agc", lower_part, grouped, preferred_element_type=jnp.float32
    )
    conv_sum = jnp.einsum("gab,agc->bgc", upper_part, grad_rows, preferred_element_type=jnp.float32)
    conv_sum = conv_sum + jnp.einsum(
        "gab,agc->bgc", lower_part, grad_rows, preferred_element_type=jnp.float32
    )
    position = jnp.arange(span).astype(jnp.float32)
    to_end = jnp.exp(-decays[:, :, None] * (span - 1.0 - position)[None, None, :])
    from_start = jnp.exp(-decays[:, :, None] * position[None, None, :])
    end_states = jnp.einsum("gmb,bgc->gmc", to_end, grouped.astype(jnp.float32), precision=HIGHEST)
    start_states = jnp.einsum(
        "gma,agc->gmc", from_start, grad_rows.astype(jnp.float32), precision=HIGHEST
    )
    factor = jnp.exp(-decays * float(span))
    carried_in, behind = carry_states(end_states, start_states, factor, span)
    rising = jnp.exp(-decays[:, :, None] * (position + 1.0)[None, None, :])
    falling = jnp.exp(-decays[:, :, None] * (span - position)[None, None, :])
    mixed_sum = mixed_sum + jnp.einsum(
        "gma,gmc->agc", term_residues[:, :, None] * rising, carried_in, precision=HIGHEST
    )
    conv_sum = conv_sum + jnp.einsum(
        "gmb,gmc->bgc", term_residues[:, :, None] * falling, behind, precision=HIGHEST
    )
    projected = jnp.einsum(
        "agc,gmc->gma", grad_rows.astype(jnp.float32), carried_in, precision=HIGHEST
    )
    residue_share = inside + jnp.sum(projected * rising, axis=2)
    return (mixed_sum.reshape(span, columns), conv_sum.reshape(span, columns), residue_share)


def finish(query_part, key_part, value_part, grad_part, mixed_out, conv_grad):
    output = query_part.astype(jnp.float32) * mixed_out
    query_grad = grad_part.astype(jnp.float32) * mixed_out
    key_grad = conv_grad * value_part.astype(jnp.float32)
    value_grad = conv_grad * key_part.astype(jnp.float32)
    return (output, query_grad, key_grad, value_grad)


def gated_inputs(query_input, key_input, value_input, out_grad):
    product = (key_input.astype(jnp.float32) * value_input.astype(jnp.float32)).astype(jnp.bfloat16)
    inner_grad = (out_grad.astype(jnp.float32) * query_input.astype(jnp.float32)).astype(
        jnp.bfloat16
    )
    return (product, inner_grad)


def channel_layout(query_input, key_input, value_input, out_grad, residues, decay_rates):
    product, inner_grad = gated_inputs(query_input, key_input, value_input, out_grad)
    prod_cols, grad_cols = (
        lax.all_to_all(product, "grp", split_axis=1, concat_axis=0, tiled=True),
        lax.all_to_all(inner_grad, "grp", split_axis=1, concat_axis=0, tiled=True),
    )
    row_count, columns = prod_cols.shape
    group_count = columns // GROUP
    first_group = lax.axis_index("grp") * group_count
    local_res = lax.dynamic_slice_in_dim(residues, first_group, group_count, 0)
    local_decay = lax.dynamic_slice_in_dim(decay_rates, first_group, group_count, 0)

    def carry_states(end_states, start_states, factor, span):
        neutral = (jnp.zeros_like(end_states), jnp.ones_like(factor))
        carried_in, spent_ahead = entering((end_states, factor), "ctx", link_states, neutral, False)
        behind, spent_behind = entering((start_states, factor), "ctx", link_states, neutral, True)
        return (carried_in, behind)

    mixed_cols, conv_cols, residue_share = convolve(
        prod_cols, grad_cols, local_res, local_decay, carry_states
    )
    mixed_rows, conv_rows = (
        lax.all_to_all(mixed_cols, "grp", split_axis=0, concat_axis=1, tiled=True),
        lax.all_to_all(conv_cols, "grp", split_axis=0, concat_axis=1, tiled=True),
    )
    results = finish(query_input, key_input, value_input, out_grad, mixed_rows, conv_rows)
    placed = lax.dynamic_update_slice_in_dim(
        jnp.zeros(residues.shape, jnp.float32), residue_share, first_group, 0
    )
    return (results, placed, row_count * lax.axis_size("ctx"))


def on_device(query_input, key_input, value_input, out_grad, residues, decay_rates):
    results, placed, length = channel_layout(
        query_input, key_input, value_input, out_grad, residues, decay_rates
    )
    summed = lax.psum(placed, ("ctx", "grp"))
    residue_grad = summed / (length * math.sqrt(GROUP))
    return (results[0], results[1], results[2], results[3], residue_grad)


def solution(mesh):
    in_specs = (
        P(("ctx", "grp"), None),
        P(("ctx", "grp"), None),
        P(("ctx", "grp"), None),
        P(("ctx", "grp"), None),
        P(),
        P(),
    )
    out_specs = (
        P(("ctx", "grp"), None),
        P(("ctx", "grp"), None),
        P(("ctx", "grp"), None),
        P(("ctx", "grp"), None),
        P(),
    )
    return jax.shard_map(
        on_device, mesh=mesh, in_specs=in_specs, out_specs=out_specs, check_vma=False
    )
```

profile of v0, /device:TPU:1, one launch (start us, length us, event | category | flops | bytes accessed | tf_op | source)
XLA Modules:
  0.0 491.0 jit_solution(2044057091201564266)
XLA Ops:
  7.2 1.8 fusion.5
  9.0 1.1 copy.101
  10.0 6.0 %all-to-all-start.1 = ((bf16[128,4,1024]{2,0,1:T(8,128)(2,1)}), bf16[128,4,1024]{2,0,1:T(8,128)(2,1)S(1)}, u32[]{:S(2)}, u32[]{:S(2)}) async-start(bf16[128,4,1024]{2,0,1:T(8,128)(2,1)} %bitcast.53), calls=%async_computation.1 | async-start | bytes 2097152 | tf_op jit(solution)/shard_map/all_to_all | solution.py:112
  16.9 14.2 %all-to-all-done.1 = bf16[128,4,1024]{2,0,1:T(8,128)(2,1)S(1)} async-done(((bf16[128,4,1024]{2,0,1:T(8,128)(2,1)}), bf16[128,4,1024]{2,0,1:T(8,128)(2,1)S(1)}, u32[]{:S(2)}, u32[]{:S(2)}) %all-to-all-start.1) | async-done | bytes 1048608 | tf_op jit(solution)/shard_map/all_to_all | solution.py:112
  32.1 1.8 reshape.76
  33.9 1.2 fusion.12
  36.5 5.1 %all-to-all-start = ((bf16[128,4,1024]{2,0,1:T(8,128)(2,1)}), bf16[128,4,1024]{2,0,1:T(8,128)(2,1)}, u32[]{:S(2)}, u32[]{:S(2)}) async-start(bf16[128,4,1024]{2,0,1:T(8,128)(2,1)} %bitcast.54), calls=%async_computation | async-start | bytes 2097152 | tf_op jit(solution)/shard_map/all_to_all | solution.py:111
  41.7 68.3 %all-gather.3 = f32[32,2,16]{2,1,0:T(2,128)S(1)} all-gather(f32[1,2,16]{2,1,0:T(2,128)S(1)} %get-tuple-element.293), channel_id=2, replica_groups=mesh['ctx'=32,'grp'=4] {'ctx'}, dimensions={0}, use_global_device_ids=true | all-gather | bytes 4224 | tf_op jit(solution)/shard_map/all_gather | solution.py:15
  110.1 2.6 reshape.75
  112.7 2.4 fusion.7
  115.1 3.3 fusion.9
  118.4 54.7 %while.43 = (s32[]{:T(128)}, f32[2,512,512]{2,1,0:T(8,128)S(1)}, f32[16,2]{1,0:T(8,128)S(1)}, f32[16,2]{1,0:T(8,128)S(1)}, f32[16,2]{1,0:T(8,128)S(1)}, /*index=...) while((s32[]{:T(128)}, f32[2,512,512]{2,1,0:T(8,128)S(1)}, ...), condition=%wide.region_2.3_spmd.clone.clone.clone, body=%wide.region_0.2_spmd.clone.clone.clone.sunk | while | flops 4718595 | bytes 8917183 | solution.py:43
  118.9 3.0 multiply_reduce_fusion.2
  122.3 3.0 multiply_reduce_fusion.2
  125.7 3.0 multiply_reduce_fusion.2
  129.1 3.0 multiply_reduce_fusion.2
  132.5 3.0 multiply_reduce_fusion.2
  135.9 3.0 multiply_reduce_fusion.2
  139.4 3.0 multiply_reduce_fusion.2
  142.8 3.0 multiply_reduce_fusion.2
  146.2 3.0 multiply_reduce_fusion.2
  149.6 3.0 multiply_reduce_fusion.2
  153.0 3.0 multiply_reduce_fusion.2
  156.4 3.0 multiply_reduce_fusion.2
  159.9 3.0 multiply_reduce_fusion.2
  163.3 3.0 multiply_reduce_fusion.2
  166.7 3.0 multiply_reduce_fusion.2
  170.1 3.0 multiply_reduce_fusion.2
  173.1 2.5 copy.78
  175.6 3.7 copy.71
  179.2 3.4 fusion.39
  182.6 2.0 fusion.43
  184.7 2.1 fusion.41
  186.7 2.1 fusion.44
  188.8 28.8 %while.42 = (s32[]{:T(128)}, f32[2,16,512]{2,1,0:T(8,128)S(1)}, s32[]{:T(128)}, f32[32,2,16]{2,1,0:T(2,128)S(1)}, f32[32,2,16,512]{3,2,1,0:T(8,128)}, /*index=5*/s32[]{:T(128)}, s32[]{:T(128)}, s32[]{:T(128)}, s32[]{:T(128)}) while((s32[]{:T(128)}, f32[2,16,512]{2,1,0:T(8,128)S(1)}, s32[]{:T(128)}, f32[32,2,16]{2,1,0:T(2,128)S(1)}, ...), condition=%wide.region_6.7_spmd, body=%wide.region_5.6_spmd.sunk | while | flops 32774 | bytes 197147 | solution.py:24
  217.6 5.5 %add_bitcast_fusion = f32[512,2,512]{0,2,1:T(8,128)} fusion(f32[2,512,512]{2,1,0:T(8,128)} %fusion.39, f32[2,512,512]{2,1,0:T(8,128)} %fusion.43, f32[2,16,512]{2,1,0:T(8,128)S(1)} %get-tuple-element.178, f32[512]{0:T(512)S(1)} %fusion.35, f32[2,16]{1,0:T(2,128)S(1)} %constant_dynamic-slice_fusion.1, f32[2,16]{1,0:T(2,128)S(1)} %get-tuple-element.294), kind=kOutput, calls=%fused_computation.21 | convolution fusion | flops 101744640 | bytes 6359296 | tf_op jit(solution)/shard_map/gmb,gmc->bgc/dot_general | solution.py:82
  223.1 1.9 all_to_all.62
  225.0 1.5 copy.81
  226.5 18.8 %all-to-all-start.3 = ((f32[4,128,1024]{1,2,0:T(8,128)}), f32[4,128,1024]{1,2,0:T(8,128)S(1)}, u32[]{:S(2)}, u32[]{:S(2)}) async-start(f32[4,128,1024]{1,2,0:T(8,128)} %copy.81), calls=%async_computation.3 | async-start | bytes 4194304 | tf_op jit(solution)/shard_map/all_to_all | solution.py:131
  245.3 77.5 %all-gather.7.cloned.1.call-done = f32[64,16,512]{2,1,0:T(8,128)} async-done(((f32[2,16,512]{2,1,0:T(8,128)}), f32[64,16,512]{2,1,0:T(8,128)}) %all-gather.7.cloned.1.call-update) | async-done | bytes 2097168 | tf_op jit(solution)/shard_map/all_gather | solution.py:15
  322.9 5.5 %add_bitcast_fusion.1 = f32[512,2,512]{0,2,1:T(8,128)} fusion(f32[2,512,512]{2,1,0:T(8,128)} %fusion.41, f32[2,512,512]{2,1,0:T(8,128)} %fusion.44, f32[2,16,512]{2,1,0:T(8,128)S(1)} %get-tuple-element.177, f32[512]{0:T(512)S(1)} %fusion.33, f32[2,16]{1,0:T(2,128)S(1)} %constant_dynamic-slice_fusion.1, f32[2,16]{1,0:T(2,128)S(1)} %get-tuple-element.294), kind=kOutput, calls=%fused_computation.22 | convolution fusion | flops 101744640 | bytes 6359296 | tf_op jit(solution)/shard_map/gma,gmc->agc/dot_general | solution.py:79
  328.4 2.9 all_to_all.58
  331.2 3.0 copy.75
  334.3 26.2 %all-to-all-start.2 = ((f32[4,128,1024]{1,2,0:T(8,128)}), f32[4,128,1024]{1,2,0:T(8,128)}, u32[]{:S(2)}, u32[]{:S(2)}) async-start(f32[4,128,1024]{1,2,0:T(8,128)} %copy.75), calls=%async_computation.2 | async-start | bytes 4194304 | tf_op jit(solution)/shard_map/all_to_all | solution.py:130
  361.6 110.7 %psum.7 = f32[8,16]{1,0:T(8,128)S(1)} all-reduce(f32[8,16]{1,0:T(8,128)S(1)} %fusion.36), channel_id=1, replica_groups=mesh['ctx'=32,'grp'=4] {'ctx','grp'}, use_global_device_ids=true, to_apply=%region_8.9 | all-reduce | flops 128 | bytes 1024 | tf_op jit(solution)/shard_map/psum | solution.py:144
  472.9 1.8 copy.82
  474.8 3.0 copy.76
  477.8 6.3 %convert_multiply_fusion = (f32[128,4096]{1,0:T(8,128)}, f32[128,4096]{1,0:T(8,128)}, f32[128,4096]{1,0:T(8,128)}, f32[128,4096]{1,0:T(8,128)}) fusion(f32[128,4096]{1,0:T(8,128)} %copy.76, bf16[128,4096]{1,0:T(8,128)(2,1)} %param.15, bf16[128,4096]{1,0:T(8,128)(2,1)} %param.12, f32[128,4096]{1,0:T(8,128)S(1)} %copy-done.3, ...), kind=kLoop, calls=%fused_computation.13 | loop fusion | flops 4194304 | bytes 16777216 | tf_op jit(solution)/shard_map/mul | solution.py:94
  (170 shorter events, 40.5 us)
Async XLA Ops:
  7.2 34.5 %copy-start = (f32[8,16]{1,0:T(8,128)S(1)}, f32[8,16]{1,0:T(8,128)}, u32[]{:S(2)}) copy-start(f32[8,16]{1,0:T(8,128)} %param.16) | copy-start | bytes 1540
  10.0 21.1 %all-to-all-start.1 = ((bf16[128,4,1024]{2,0,1:T(8,128)(2,1)}), bf16[128,4,1024]{2,0,1:T(8,128)(2,1)S(1)}, u32[]{:S(2)}, u32[]{:S(2)}) async-start(bf16[128,4,1024]{2,0,1:T(8,128)(2,1)} %bitcast.53), calls=%async_computation.1 | async-start | bytes 2097152 | tf_op jit(solution)/shard_map/all_to_all | solution.py:112
  16.0 19.1 %copy-start.4 = (bf16[128,4096]{1,0:T(8,128)(2,1)S(1)}, bf16[128,4096]{1,0:T(8,128)(2,1)}, u32[]{:S(2)}) copy-start(bf16[128,4096]{1,0:T(8,128)(2,1)} %param.14) | copy-start | bytes 3145732
  16.0 19.2 %copy-start.6 = (bf16[128,4096]{1,0:T(8,128)(2,1)S(1)}, bf16[128,4096]{1,0:T(8,128)(2,1)}, u32[]{:S(2)}) copy-start(bf16[128,4096]{1,0:T(8,128)(2,1)} %param.13) | copy-start | bytes 3145732
  16.0 172.8 %all-gather.9.cloned.1.call-start = ((), (), s32[]{:S(2)}) async-start(), calls=%async_computation.5 | async-start | bytes 2162688 | tf_op jit(solution)/shard_map/all_gather | solution.py:15
  31.1 1.0 copy-start.7
  36.5 73.6 %all-to-all-start = ((bf16[128,4,1024]{2,0,1:T(8,128)(2,1)}), bf16[128,4,1024]{2,0,1:T(8,128)(2,1)}, u32[]{:S(2)}, u32[]{:S(2)}) async-start(bf16[128,4,1024]{2,0,1:T(8,128)(2,1)} %bitcast.54), calls=%async_computation | async-start | bytes 2097152 | tf_op jit(solution)/shard_map/all_to_all | solution.py:111
  41.6 281.3 %all-gather.7.cloned.1.call-start = ((), (), s32[]{:S(2)}) async-start(), calls=%async_computation.4 | async-start | bytes 2162688 | tf_op jit(solution)/shard_map/all_gather | solution.py:15
  179.2 3.4 copy-start.2
  182.6 2.1 copy-start.1
  226.5 107.8 %all-to-all-start.3 = ((f32[4,128,1024]{1,2,0:T(8,128)}), f32[4,128,1024]{1,2,0:T(8,128)S(1)}, u32[]{:S(2)}, u32[]{:S(2)}) async-start(f32[4,128,1024]{1,2,0:T(8,128)} %copy.81), calls=%async_computation.3 | async-start | bytes 4194304 | tf_op jit(solution)/shard_map/all_to_all | solution.py:131
  334.3 140.5 %all-to-all-start.2 = ((f32[4,128,1024]{1,2,0:T(8,128)}), f32[4,128,1024]{1,2,0:T(8,128)}, u32[]{:S(2)}, u32[]{:S(2)}) async-start(f32[4,128,1024]{1,2,0:T(8,128)} %copy.75), calls=%async_computation.2 | async-start | bytes 4194304 | tf_op jit(solution)/shard_map/all_to_all | solution.py:130
  474.8 3.0 copy-start.3
  474.8 3.0 copy-start.5
Sparse Core Ops, SparseCore 0:
  35.3 132.3 all-gather.8
  169.3 153.5 all-gather.6
where the time goes:
time: 494 us; the launch traced here: 491 us
  blocking collectives  179 us (36%)
  other arithmetic  91.8 us (19%)
  waiting for transfers between devices  91.8 us (19%)
  starting transfers between devices  56.1 us (11%)
  local copies, waits for them, and re-layouts  28.8 us (6%)
  matrix products  28.5 us (6%)
  between operations  14.1 us (3%)
    psum x1, blocking collectives, on_device(): summed = lax.psum(placed, ('ctx', 'grp'))  111 us
    all_gather x2, waiting for transfers between devices, entering(): gathered = jax.tree.map(lambda a: lax.all_gather(a, axis), part)  77.6 us
    all_gather x1, blocking collectives, entering(): gathered = jax.tree.map(lambda a: lax.all_gather(a, axis), part)  68.3 us
    reduce_sum x16, other arithmetic, one_mode(): return (total, jnp.sum(pairing * weight, axis=(1, 2)))  47.3 us
    add x31, other arithmetic, link_states(): return (later[1][:, :, None] * earlier[0] + later[0], earlier[1] * later[1])  28.6 us
    all_to_all x1, starting transfers between devices, channel_layout(): lax.all_to_all(mixed_cols, 'grp', split_axis=0, concat_axis=1, tiled=True)  26.2 us
    all_to_all x1, starting transfers between devices, channel_layout(): lax.all_to_all(conv_cols, 'grp', split_axis=0, concat_axis=1, tiled=True)  18.8 us
    all_to_all x1, waiting for transfers between devices, channel_layout(): lax.all_to_all(inner_grad, 'grp', split_axis=1, concat_axis=0, tiled=True)  14.2 us
  transfers between devices with their start and end apart: 6, of which 2 were waited for; matrix products, arithmetic and copies ran while one was open for 26% of the time, Pallas kernels for 0%

commit v1 on v0

--- a/solution.py
+++ b/solution.py
@@ -6,6 +6,11 @@
 
 GROUP = 512
 HIGHEST = lax.Precision.HIGHEST
+
+
+def gather_and_add(x, mesh_axis):
+    parts = lax.all_gather(x, mesh_axis)
+    return jnp.sum(parts, axis=0)
 
 
 def entering(part, axis, combine, identity, reverse):
@@ -141,7 +146,7 @@
     results, placed, length = channel_layout(
         query_input, key_input, value_input, out_grad, residues, decay_rates
     )
-    summed = lax.psum(placed, ("ctx", "grp"))
+    summed = gather_and_add(placed, ("ctx", "grp"))
     residue_grad = summed / (length * math.sqrt(GROUP))
     return (results[0], results[1], results[2], results[3], residue_grad)
 

time: 494 us -> 605 us (1.22)
  blocking collectives: 179 us -> 290 us
    all_gather x0 -> x1, blocking collectives: none -> 222 us  [gather_and_add(): parts = lax.all_gather(x, mesh_axis)]
    psum x1 -> x0, blocking collectives: 111 us -> none  [on_device(): summed = lax.psum(placed, ('ctx', 'grp'))]
  transfers between devices with their start and end apart: 6 -> 6, of which waited for: 2 -> 2; matrix products, arithmetic and copies ran while one was open for 26% -> 21% of each run, Pallas kernels for 0% -> 0%
where the time goes in v1:
time: 605 us; the launch traced here: 602 us
  blocking collectives  290 us (48%)
  other arithmetic  92 us (15%)
  waiting for transfers between devices  91.8 us (15%)
  starting transfers between devices  56.1 us (9%)
  local copies, waits for them, and re-layouts  28.8 us (5%)
  matrix products  28.5 us (5%)
  between operations  14.1 us (2%)
    all_gather x1, blocking collectives, gather_and_add(): parts = lax.all_gather(x, mesh_axis)  222 us
    all_gather x2, waiting for transfers between devices, entering(): gathered = jax.tree.map(lambda a: lax.all_gather(a, axis), part)  77.6 us
    all_gather x1, blocking collectives, entering(): gathered = jax.tree.map(lambda a: lax.all_gather(a, axis), part)  68.3 us
    reduce_sum x16, other arithmetic, one_mode(): return (total, jnp.sum(pairing * weight, axis=(1, 2)))  47.3 us
    add x31, other arithmetic, link_states(): return (later[1][:, :, None] * earlier[0] + later[0], earlier[1] * later[1])  28.6 us
    all_to_all x1, starting transfers between devices, channel_layout(): lax.all_to_all(mixed_cols, 'grp', split_axis=0, concat_axis=1, tiled=True)  26.2 us
    all_to_all x1, starting transfers between devices, channel_layout(): lax.all_to_all(conv_cols, 'grp', split_axis=0, concat_axis=1, tiled=True)  18.8 us
    all_to_all x1, waiting for transfers between devices, channel_layout(): lax.all_to_all(inner_grad, 'grp', split_axis=1, concat_axis=0, tiled=True)  14.2 us
  transfers between devices with their start and end apart: 6, of which 2 were waited for; matrix products, arithmetic and copies ran while one was open for 21% of the time, Pallas kernels for 0%

profile of v1, /device:TPU:1, one launch (start us, length us, event | category | flops | bytes accessed | tf_op | source)
XLA Modules:
  0.0 602.2 jit_solution(5596245123580601130)
XLA Ops:
  7.2 1.8 fusion.5
  9.0 1.1 copy.101
  10.0 6.0 all-to-all-start.1
  16.9 14.2 %all-to-all-done.1 = bf16[128,4,1024]{2,0,1:T(8,128)(2,1)S(1)} async-done(((bf16[128,4,1024]{2,0,1:T(8,128)(2,1)}), bf16[128,4,1024]{2,0,1:T(8,128)(2,1)S(1)}, u32[]{:S(2)}, u32[]{:S(2)}) %all-to-all-start.1) | async-done | bytes 1048608 | tf_op jit(solution)/shard_map/all_to_all | solution.py:117
  32.1 1.8 reshape.78
  33.9 1.2 fusion.12
  36.5 5.1 all-to-all-start
  41.7 68.3 %all-gather.3 = f32[32,2,16]{2,1,0:T(2,128)S(1)} all-gather(f32[1,2,16]{2,1,0:T(2,128)S(1)} %get-tuple-element.293), channel_id=2, replica_groups=mesh['ctx'=32,'grp'=4] {'ctx'}, dimensions={0}, use_global_device_ids=true | all-gather | bytes 4224 | tf_op jit(solution)/shard_map/all_gather | solution.py:20
  110.1 2.6 reshape.77
  112.7 2.4 fusion.7
  115.1 3.3 fusion.9
  118.4 54.7 %while.43 = (s32[]{:T(128)}, f32[2,512,512]{2,1,0:T(8,128)S(1)}, f32[16,2]{1,0:T(8,128)S(1)}, f32[16,2]{1,0:T(8,128)S(1)}, f32[16,2]{1,0:T(8,128)S(1)}, /*index=...) while((s32[]{:T(128)}, f32[2,512,512]{2,1,0:T(8,128)S(1)}, ...), condition=%wide.region_2.3_spmd.clone.clone.clone, body=%wide.region_0.2_spmd.clone.clone.clone.sunk | while | flops 4718595 | bytes 8917183 | solution.py:48
  118.9 3.0 multiply_reduce_fusion.2
  122.3 3.0 multiply_reduce_fusion.2
  125.7 3.0 multiply_reduce_fusion.2
  129.1 3.0 multiply_reduce_fusion.2
  132.5 3.0 multiply_reduce_fusion.2
  135.9 3.0 multiply_reduce_fusion.2
  139.4 3.0 multiply_reduce_fusion.2
  142.8 3.0 multiply_reduce_fusion.2
  146.2 3.0 multiply_reduce_fusion.2
  149.6 3.0 multiply_reduce_fusion.2
  153.0 3.0 multiply_reduce_fusion.2
  156.4 3.0 multiply_reduce_fusion.2
  159.9 3.0 multiply_reduce_fusion.2
  163.3 3.0 multiply_reduce_fusion.2
  166.7 3.0 multiply_reduce_fusion.2
  170.1 3.0 multiply_reduce_fusion.2
  173.1 2.5 copy.78
  175.6 3.7 copy.71
  179.2 3.4 fusion.38
  182.6 2.0 fusion.42
  184.7 2.1 fusion.40
  186.7 2.1 fusion.43
  188.8 28.8 %while.42 = (s32[]{:T(128)}, f32[2,16,512]{2,1,0:T(8,128)S(1)}, s32[]{:T(128)}, f32[32,2,16]{2,1,0:T(2,128)S(1)}, f32[32,2,16,512]{3,2,1,0:T(8,128)}, /*index=5*/s32[]{:T(128)}, s32[]{:T(128)}, s32[]{:T(128)}, s32[]{:T(128)}) while((s32[]{:T(128)}, f32[2,16,512]{2,1,0:T(8,128)S(1)}, s32[]{:T(128)}, f32[32,2,16]{2,1,0:T(2,128)S(1)}, ...), condition=%wide.region_6.7_spmd, body=%wide.region_5.6_spmd.sunk | while | flops 32774 | bytes 197147 | solution.py:29
  217.6 5.5 add_bitcast_fusion
  223.1 1.9 all_to_all.62
  225.0 1.5 copy.81
  226.5 18.8 %all-to-all-start.3 = ((f32[4,128,1024]{1,2,0:T(8,128)}), f32[4,128,1024]{1,2,0:T(8,128)S(1)}, u32[]{:S(2)}, u32[]{:S(2)}) async-start(f32[4,128,1024]{1,2,0:T(8,128)} %copy.81), calls=%async_computation.3 | async-start | bytes 4194304 | tf_op jit(solution)/shard_map/all_to_all | solution.py:136
  245.3 77.5 %all-gather.7.cloned.1.call-done = f32[64,16,512]{2,1,0:T(8,128)} async-done(((f32[2,16,512]{2,1,0:T(8,128)}), f32[64,16,512]{2,1,0:T(8,128)}) %all-gather.7.cloned.1.call-update) | async-done | bytes 2097168 | tf_op jit(solution)/shard_map/all_gather | solution.py:20
  322.9 5.5 add_bitcast_fusion.1
  328.4 2.9 all_to_all.58
  331.2 3.0 copy.75
  334.3 26.2 %all-to-all-start.2 = ((f32[4,128,1024]{1,2,0:T(8,128)}), f32[4,128,1024]{1,2,0:T(8,128)}, u32[]{:S(2)}, u32[]{:S(2)}) async-start(f32[4,128,1024]{1,2,0:T(8,128)} %copy.75), calls=%async_computation.2 | async-start | bytes 4194304 | tf_op jit(solution)/shard_map/all_to_all | solution.py:135
  361.6 221.9 %all_gather.33 = f32[128,8,16]{2,1,0:T(8,128)S(1)} all-gather(f32[1,8,16]{2,1,0:T(8,128)S(1)} %bitcast_dynamic-update-slice_fusion), channel_id=1, replica_groups=mesh['ctx'=32,'grp'=4] {'ctx','grp'}, dimensions={0}, use_global_device_ids=true | all-gather | bytes 66048 | tf_op jit(solution)/shard_map/all_gather | solution.py:12
  584.2 1.8 copy.82
  586.0 3.0 copy.76
  589.1 6.3 %convert_multiply_fusion = (f32[128,4096]{1,0:T(8,128)}, f32[128,4096]{1,0:T(8,128)}, f32[128,4096]{1,0:T(8,128)}, f32[128,4096]{1,0:T(8,128)}) fusion(f32[128,4096]{1,0:T(8,128)} %copy.76, bf16[128,4096]{1,0:T(8,128)(2,1)} %param.15, bf16[128,4096]{1,0:T(8,128)(2,1)} %param.12, f32[128,4096]{1,0:T(8,128)S(1)} %copy-done.3, ...), kind=kLoop, calls=%fused_computation.13 | loop fusion | flops 4194304 | bytes 16777216 | tf_op jit(solution)/shard_map/mul | solution.py:99
  (171 shorter events, 40.6 us)
Async XLA Ops:
  7.2 34.5 %copy-start = (f32[8,16]{1,0:T(8,128)S(1)}, f32[8,16]{1,0:T(8,128)}, u32[]{:S(2)}) copy-start(f32[8,16]{1,0:T(8,128)} %param.16) | copy-start | bytes 1540
  10.0 21.1 %all-to-all-start.1 = ((bf16[128,4,1024]{2,0,1:T(8,128)(2,1)}), bf16[128,4,1024]{2,0,1:T(8,128)(2,1)S(1)}, u32[]{:S(2)}, u32[]{:S(2)}) async-start(bf16[128,4,1024]{2,0,1:T(8,128)(2,1)} %bitcast.55), calls=%async_computation.1 | async-start | bytes 2097152 | tf_op jit(solution)/shard_map/all_to_all | solution.py:117
  16.0 19.1 %copy-start.4 = (bf16[128,4096]{1,0:T(8,128)(2,1)S(1)}, bf16[128,4096]{1,0:T(8,128)(2,1)}, u32[]{:S(2)}) copy-start(bf16[128,4096]{1,0:T(8,128)(2,1)} %param.14) | copy-start | bytes 3145732
  16.0 19.2 %copy-start.6 = (bf16[128,4096]{1,0:T(8,128)(2,1)S(1)}, bf16[128,4096]{1,0:T(8,128)(2,1)}, u32[]{:S(2)}) copy-start(bf16[128,4096]{1,0:T(8,128)(2,1)} %param.13) | copy-start | bytes 3145732
  16.0 172.8 %all-gather.9.cloned.1.call-start = ((), (), s32[]{:S(2)}) async-start(), calls=%async_computation.5 | async-start | bytes 2162688 | tf_op jit(solution)/shard_map/all_gather | solution.py:20
  31.1 1.0 copy-start.7
  36.5 73.6 %all-to-all-start = ((bf16[128,4,1024]{2,0,1:T(8,128)(2,1)}), bf16[128,4,1024]{2,0,1:T(8,128)(2,1)}, u32[]{:S(2)}, u32[]{:S(2)}) async-start(bf16[128,4,1024]{2,0,1:T(8,128)(2,1)} %bitcast.56), calls=%async_computation | async-start | bytes 2097152 | tf_op jit(solution)/shard_map/all_to_all | solution.py:116
  41.6 281.3 %all-gather.7.cloned.1.call-start = ((), (), s32[]{:S(2)}) async-start(), calls=%async_computation.4 | async-start | bytes 2162688 | tf_op jit(solution)/shard_map/all_gather | solution.py:20
  179.2 3.4 copy-start.2
  182.6 2.1 copy-start.1
  226.5 107.8 %all-to-all-start.3 = ((f32[4,128,1024]{1,2,0:T(8,128)}), f32[4,128,1024]{1,2,0:T(8,128)S(1)}, u32[]{:S(2)}, u32[]{:S(2)}) async-start(f32[4,128,1024]{1,2,0:T(8,128)} %copy.81), calls=%async_computation.3 | async-start | bytes 4194304 | tf_op jit(solution)/shard_map/all_to_all | solution.py:136
  334.3 251.7 %all-to-all-start.2 = ((f32[4,128,1024]{1,2,0:T(8,128)}), f32[4,128,1024]{1,2,0:T(8,128)}, u32[]{:S(2)}, u32[]{:S(2)}) async-start(f32[4,128,1024]{1,2,0:T(8,128)} %copy.75), calls=%async_computation.2 | async-start | bytes 4194304 | tf_op jit(solution)/shard_map/all_to_all | solution.py:135
  586.0 3.0 copy-start.3
  586.0 3.0 copy-start.5
Sparse Core Ops, SparseCore 0:
  35.3 132.3 all-gather.8
  169.3 153.5 all-gather.6
